TPU v7x, 256 devices: a whole 4x4x8 slice. The times are simulated.
256 devices in a mesh: req: 64 (over x, z, core), tp: 4 (over y).
Axes of the slice: x: 4, y: 4, z: 8, core: 2. Of those that a mesh axis runs over, the one named last changes fastest.
Arguments:
- hidden_in: bfloat16 [512, 1600], P('req'), may hold values from -6 to 6
- norm_gain: float32 [1600], replicated, may hold values from 0.1 to 1.9
- query_weight: bfloat16 [1600, 1280], P(None, 'tp'), may hold values from -0.15625 to 0.15625
- memory_weight: bfloat16 [1600, 512], P(None, 'tp'), may hold values from -0.15625 to 0.15625
- attention_out: bfloat16 [1280, 1600], P('tp'), may hold values from -0.15625 to 0.15625
- attention_gain: float32 [1280], P('tp'), may hold values from 0.1 to 1.9
- mamba_input: bfloat16 [2, 1600, 1600], P(None, None, 'tp'), may hold values from -0.15625 to 0.15625
- conv_weight: float32 [4, 1600], P(None, 'tp'), may hold values from -3 to 3
- conv_state: bfloat16 [512, 3, 1600], P('req', None, 'tp'), may hold values from -6 to 6
- select_weight: bfloat16 [1600, 132], P('tp'), may hold values from -0.15625 to 0.15625
- step_weight: bfloat16 [100, 1600], P(None, 'tp'), may hold values from -0.625 to 0.625
- step_bias: float32 [1600], P('tp'), may hold values from -4 to -1
- decay_log: float32 [16, 1600], P(None, 'tp'), may hold values from 0 to 2.77
- skip_gain: float32 [1600], P('tp'), may hold values from 0.5 to 1.5
- scan_state: float32 [512, 16, 1600], P('req', None, 'tp'), may hold values from -6 to 6
- mamba_gain: float32 [1600], P('tp'), may hold values from 0.1 to 1.9
- mamba_out: bfloat16 [1600, 1600], P('tp'), may hold values from -0.15625 to 0.15625
- cache_blocks: bfloat16 [2176, 4, 512, 128], P('req', 'tp'), as said below
- lengths: int32 [512], replicated, may hold values from 257 to 8192, as said below
- slot_request: int32 [2176], P('req'), may hold values from -1 to 511, as said below
- slot_block: int32 [2176], P('req'), may hold values from 0 to 15, as said below
Outputs:
- layer_out: bfloat16 [512, 1600], P('req', 'tp')
- new_state: float32 [512, 16, 1600], P('req', None, 'tp')
Inputs may be any that keep to these rules, and one draw needn't show every extreme that they name: `lengths`: some request holds exactly 8192 tokens. `slot_request`: -1 marks an empty slot; a request with L cached tokens fills exactly ceil(L / 512) slots; the slots of one index of req hold at most 2 blocks of the requests of any one index of req (requests r with equal r // 8), and some index of req holds exactly 2. `slot_block`: the slots of one request carry its block numbers 0 to ceil(L / 512) - 1, each once; empty slots carry 0. `cache_blocks`: the first 64 entries of the last dimension are keys, the rest values.
All inputs are finite; a program needn't handle non-finite values.
Results may differ from a plain program's by a relative error of at most 0.012.
Values may be sent and summed in bfloat16 or wider, within the bound.
A program may use at most 64 MiB of HBM per device.

v0:
```python
import jax
import jax.numpy as jnp
from jax import lax
from jax.sharding import PartitionSpec as P

HQ = 20
HD = 64
MI = 1600


def rotate_pairs(vector, position):
    head_dim = vector.shape[-1]
    half_dim = head_dim // 2
    frequency = jnp.power(
        jnp.float32(10000.0), -jnp.arange(half_dim, dtype=jnp.float32) * (2.0 / head_dim)
    )
    angles = position.astype(jnp.float32)[:, None, None] * frequency
    cosine = jnp.cos(angles)
    sine_part = jnp.sin(angles)
    front_half = vector[..., :half_dim]
    back_half = vector[..., half_dim:]
    return jnp.concatenate(
        [front_half * cosine - back_half * sine_part, back_half * cosine + front_half * sine_part],
        -1,
    )


def body(
    hidden_in,
    norm_gain,
    query_weight,
    memory_weight,
    attention_out,
    attention_gain,
    mamba_input,
    conv_weight,
    conv_state,
    select_weight,
    step_weight,
    step_bias,
    decay_log,
    skip_gain,
    scan_state,
    mamba_gain,
    mamba_out,
    cache_blocks,
    lengths,
    slot_request,
    slot_block,
):
    row_count = hidden_in.shape[0]
    model_width = hidden_in.shape[1]
    head_dim = cache_blocks.shape[3] // 2
    head_count = query_weight.shape[1] // head_dim
    block_len = cache_blocks.shape[2]
    slot_count = cache_blocks.shape[0]
    request_count = lengths.shape[0]
    holders = lax.axis_size("req")
    tp_count = lax.axis_size("tp")
    own_first = lax.axis_index("req") * row_count
    own_len = lax.dynamic_slice_in_dim(lengths, own_first, row_count)
    hidden_f = hidden_in.astype(jnp.float32)
    normed = (
        hidden_f * lax.rsqrt(jnp.mean(hidden_f * hidden_f, -1, keepdims=True) + 1e-06) * norm_gain
    ).astype(jnp.bfloat16)
    query_raw = jnp.dot(normed, query_weight, preferred_element_type=jnp.float32).reshape(
        row_count, head_count, head_dim
    )
    query = rotate_pairs(query_raw, own_len).astype(jnp.bfloat16)
    memory = jnp.dot(normed, memory_weight, preferred_element_type=jnp.float32)
    key_new = rotate_pairs(memory[:, None, :head_dim], own_len).astype(jnp.bfloat16)
    value_new = memory[:, head_dim:].astype(jnp.bfloat16)
    all_query = lax.all_gather(
        query.reshape(row_count, head_count * head_dim), "req", axis=0, tiled=True
    )
    slot_used = slot_request >= 0
    owner_row = jnp.where(slot_used, slot_request, 0)
    slot_query = jnp.take(all_query, owner_row, axis=0).reshape(slot_count, head_count, head_dim)
    keys = cache_blocks[:, 0, :, :head_dim]
    values = cache_blocks[:, 0, :, head_dim:]
    valid_len = jnp.where(slot_used, jnp.take(lengths, owner_row) - slot_block * block_len, 0)
    live_mask = jnp.arange(block_len)[None, :] < valid_len[:, None]
    scores = jnp.einsum(
        "shd,std->sht", slot_query, keys, preferred_element_type=jnp.float32
    ) * head_dim ** (-0.5)
    scores = jnp.where(live_mask[:, None, :], scores, -1e30)
    block_max = jnp.max(scores, 2)
    weights = jnp.where(live_mask[:, None, :], jnp.exp(scores - block_max[..., None]), 0.0).astype(
        jnp.bfloat16
    )
    block_sum = jnp.sum(weights.astype(jnp.float32), 2)
    block_out = jnp.einsum("sht,std->shd", weights, values, preferred_element_type=jnp.float32)
    own_score = jnp.sum(query.astype(jnp.float32) * key_new.astype(jnp.float32), -1) * head_dim ** (
        -0.5
    )
    value_own = value_new.astype(jnp.float32)[:, None, :]
    owner_match = slot_request[:, None] == jnp.arange(request_count)[None, :]
    request_max = jnp.max(jnp.where(owner_match[:, :, None], block_max[:, None, :], -1e30), axis=0)
    owner_table = owner_match.astype(jnp.float32)
    rescale = jnp.exp(block_max - jnp.take(request_max, owner_row, axis=0))
    scaled_out = (block_out * rescale[..., None]).reshape(slot_count, head_count * head_dim)
    part_out = jnp.dot(owner_table.T, scaled_out, precision=lax.Precision.HIGHEST)
    part_sum = jnp.dot(owner_table.T, block_sum * rescale, precision=lax.Precision.HIGHEST)
    part_out, part_sum = (part_out, part_sum)
    got_out, got_sum, got_max = (
        lax.all_to_all(
            part_out.reshape(holders, row_count, head_count * head_dim),
            "req",
            split_axis=0,
            concat_axis=0,
            tiled=True,
        ),
        lax.all_to_all(
            part_sum.reshape(holders, row_count, head_count),
            "req",
            split_axis=0,
            concat_axis=0,
            tiled=True,
        ),
        lax.all_to_all(
            request_max.reshape(holders, row_count, head_count),
            "req",
            split_axis=0,
            concat_axis=0,
            tiled=True,
        ),
    )
    top = jnp.maximum(jnp.max(got_max, 0), own_score)
    source_weight = jnp.exp(got_max - top[None])
    numer = jnp.sum(
        got_out.reshape(holders, row_count, head_count, head_dim) * source_weight[..., None], 0
    )
    denom = jnp.sum(got_sum * source_weight, 0)
    own_weight = jnp.exp(own_score - top)
    numer = numer + own_weight[..., None] * value_own
    denom = denom + own_weight
    attention = (numer / denom[..., None]).reshape(row_count, head_count * head_dim)
    mamba_x = jnp.dot(normed, mamba_input[0], preferred_element_type=jnp.float32).astype(
        jnp.bfloat16
    )
    gate_branch = jnp.dot(normed, mamba_input[1], preferred_element_type=jnp.float32)
    taps = conv_weight.shape[0]
    conv_sum = conv_weight[taps - 1] * mamba_x.astype(jnp.float32)
    for tap_index in range(taps - 1):
        conv_sum = conv_sum + conv_weight[tap_index] * conv_state[:, tap_index].astype(jnp.float32)
    activated = jax.nn.silu(conv_sum).astype(jnp.bfloat16)
    selection = lax.psum(
        jnp.dot(activated, select_weight, preferred_element_type=jnp.float32), "tp"
    )
    rank_width = step_weight.shape[0]
    state_width = decay_log.shape[0]
    step_rank = selection[:, :rank_width].astype(jnp.bfloat16)
    input_map = selection[:, rank_width : rank_width + state_width]
    output_map = selection[:, rank_width + state_width :]
    step_size = jax.nn.softplus(
        jnp.dot(step_rank, step_weight, preferred_element_type=jnp.float32) + step_bias
    )
    active_f = activated.astype(jnp.float32)
    new_state = (
        jnp.exp(-step_size[:, None, :] * jnp.exp(decay_log)[None]) * scan_state
        + step_size[:, None, :] * input_map[:, :, None] * active_f[:, None, :]
    )
    mamba_y = (jnp.sum(output_map[:, :, None] * new_state, 1) + skip_gain * active_f) * jax.nn.silu(
        gate_branch
    )
    attn_square = jnp.sum(attention * attention, -1)
    mamba_square = jnp.sum(mamba_y * mamba_y, -1)
    attn_used = (attention * attention_gain).astype(jnp.bfloat16)
    mamba_used = (mamba_y * mamba_gain).astype(jnp.bfloat16)
    attn_proj = jnp.dot(attn_used, attention_out, preferred_element_type=jnp.float32)
    mamba_proj = jnp.dot(mamba_used, mamba_out, preferred_element_type=jnp.float32)
    attn_total, mamba_total = lax.psum((attn_square, mamba_square), "tp")
    attn_scale = jnp.sqrt(attn_total / (HQ * HD) + 1e-06)
    mamba_scale = jnp.sqrt(mamba_total / MI + 1e-06)
    partial_value = 0.5 * (attn_proj / attn_scale[:, None] + mamba_proj / mamba_scale[:, None])
    mixed = lax.psum_scatter(partial_value, "tp", scatter_dimension=1, tiled=True)
    column_width = model_width // tp_count
    residual = lax.dynamic_slice_in_dim(
        hidden_f, lax.axis_index("tp") * column_width, column_width, 1
    )
    layer_out = (residual + mixed).astype(jnp.bfloat16)
    return (layer_out, new_state)


def solution(mesh):
    return jax.shard_map(
        body,
        mesh=mesh,
        in_specs=(
            P("req", None),
            P(),
            P(None, "tp"),
            P(None, "tp"),
            P("tp", None),
            P("tp"),
            P(None, None, "tp"),
            P(None, "tp"),
            P("req", None, "tp"),
            P("tp", None),
            P(None, "tp"),
            P("tp"),
            P(None, "tp"),
            P("tp"),
            P("req", None, "tp"),
            P("tp"),
            P("tp", None),
            P("req", "tp", None, None),
            P(),
            P("req"),
            P("req"),
        ),
        out_specs=(P("req", "tp"), P("req", None, "tp")),
        check_vma=False,
    )
```

profile of v0, /device:TPU:2, one launch (start us, length us, event | category | flops | bytes accessed | tf_op | source)
XLA Modules:
  0.0 191.9 jit_solution(11031688939695422736)
XLA Ops:
  7.2 0.8 compare_and_fusion
  8.0 0.7 iota_compare_fusion
  8.7 0.9 multiply_reduce_fusion.3
  9.6 1.3 fusion.74
  10.9 0.8 dynamic-slice_convert_fusion
  11.6 0.1 multiply_cosine_fusion.1
  11.7 0.1 fusion.65
  11.9 1.7 fusion.69
  13.5 0.1 reshape.303
  13.7 0.1 multiply_subtract_fusion
  13.8 0.2 multiply_reduce_fusion.4
  14.0 0.1 convert_element_type.89
  14.0 50.3 %all_gather.3 = bf16[512,320]{1,0:T(8,128)(2,1)S(1)} all-gather(bf16[8,320]{1,0:T(8,128)(2,1)S(1)} %convert_element_type.89), channel_id=1, replica_groups=mesh['req'=64,'tp'=4] {'req'}, dimensions={0}, use_global_device_ids=true | all-gather | bytes 332800 | tf_op jit(solution)/shard_map/all_gather | solution.py:73
  64.3 0.8 gather_fusion
  65.1 0.6 gather_fusion.1
  65.8 0.1 gather.16
  65.9 0.1 iota_compare_fusion.1
  66.0 3.6 %fusion.73 = (f32[34,5]{1,0:T(8,128)S(1)}, f32[34,5,512]{2,1,0:T(8,128)S(1)}) fusion(bf16[34,1,512,128]{3,2,1,0:T(8,128)(2,1)} %param.38, bf16[34,5,64]{2,1,0:T(8,128)(2,1)S(1)} %gather.16, pred[34]{0:T(512)(128)(4,1)S(1)} %get-tuple-element.14, pred[34,512]{1,0:T(8,128)(4,1)S(1)} %iota_compare_fusion.1), kind=kOutput, calls=%fused_computation.108 | convolution fusion | flops 11412950 | bytes 4844490 | tf_op jit(solution)/shard_map/shd,std->sht/dot_general | solution.py:83
  69.6 0.1 copy.65
  69.7 0.1 select_reduce_fusion
  69.9 0.1 copy.66
  70.0 0.6 gather_fusion.2
  70.6 0.1 subtract_exponential_fusion.1
  70.7 0.3 convert_reduce_fusion
  71.0 0.2 fusion.48
  71.2 0.1 reshape.306
  71.3 0.8 copy.72
  72.1 8.1 %all-to-all-start.2 = ((f32[64,8,5]{1,2,0:T(8,128)}), f32[64,8,5]{1,2,0:T(8,128)S(1)}, u32[]{:S(2)}, u32[]{:S(2)}) async-start(f32[64,8,5]{1,2,0:T(8,128)} %copy.72), calls=%async_computation.2 | async-start | bytes 524288 | tf_op jit(solution)/shard_map/all_to_all | solution.py:113
  80.3 3.7 %fusion.20 = f32[34,5,64]{2,1,0:T(8,128)S(1)} fusion(bf16[34,1,512,128]{3,2,1,0:T(8,128)(2,1)} %param.38, f32[34,5]{1,0:T(8,128)S(1)} %subtract_exponential_fusion.1, f32[34,5,512]{2,1,0:T(8,128)S(1)} %get-tuple-element.29, f32[34,5]{1,0:T(8,128)S(1)} %get-tuple-element.28, pred[34,512]{1,0:T(8,128)(4,1)S(1)} %iota_compare_fusion.1), kind=kOutput, calls=%fused_computation.21 | convolution fusion | flops 11413120 | bytes 4866896 | tf_op jit(solution)/shard_map/sht,std->shd/dot_general | solution.py:92
  84.0 0.1 reshape.337
  84.2 1.8 fusion.75
  86.1 0.1 fusion.77
  86.2 10.8 %psum.22 = f32[8,132]{1,0:T(8,128)S(1)} all-reduce(f32[8,132]{1,0:T(8,128)S(1)} %fusion.77), channel_id=1, replica_groups=mesh['req'=64,'tp'=4] {'tp'}, use_global_device_ids=true, to_apply=%region_10.11 | all-reduce | flops 1056 | bytes 8448 | tf_op jit(solution)/shard_map/psum | solution.py:147
  97.1 1.4 fusion.41
  98.5 0.2 fusion.76
  98.7 0.1 reshape.305
  98.8 0.8 copy.67
  99.7 10.3 %all-to-all-start.1 = ((f32[64,8,5]{1,2,0:T(8,128)}), f32[64,8,5]{1,2,0:T(8,128)S(1)}, u32[]{:S(2)}, u32[]{:S(2)}) async-start(f32[64,8,5]{1,2,0:T(8,128)} %copy.67), calls=%async_computation.1 | async-start | bytes 524288 | tf_op jit(solution)/shard_map/all_to_all | solution.py:120
  110.0 0.9 multiply_reduce_fusion.1
  110.9 10.7 %all-to-all-done.1 = f32[64,8,5]{1,2,0:T(8,128)S(1)} async-done(((f32[64,8,5]{1,2,0:T(8,128)}), f32[64,8,5]{1,2,0:T(8,128)S(1)}, u32[]{:S(2)}, u32[]{:S(2)}) %all-to-all-start.1) | async-done | bytes 10272 | tf_op jit(solution)/shard_map/all_to_all | solution.py:120
  121.6 6.5 %all-to-all-start = ((f32[64,8,320]{2,1,0:T(8,128)}), f32[64,8,320]{2,1,0:T(8,128)S(1)}, u32[]{:S(2)}, u32[]{:S(2)}) async-start(f32[64,8,320]{2,1,0:T(8,128)} %fusion.41), calls=%async_computation | async-start | bytes 1572864 | tf_op jit(solution)/shard_map/all_to_all | solution.py:106
  128.2 0.1 copy.68
  128.3 1.9 %multiply_reduce_fusion.5 = (f32[8]{0:T(128)S(1)}, f32[8,400]{1,0:T(8,128)S(1)}) fusion(bf16[2,1600,400]{1,2,0:T(8,128)(2,1)} %param.27, f32[1600]{0:T(1024)S(1)} %copy-done.7, f32[8]{0:T(128)S(1)} %add_rsqrt_fusion, bf16[8,1600]{1,0:T(8,128)(2,1)S(1)} %copy-done.3, f32[8,400]{1,0:T(8,128)S(1)} %get-tuple-element.4, ...), kind=kOutput, calls=%fused_computation.61 | convolution fusion | flops 10323192 | bytes 1396864 | tf_op jit(solution)/shard_map/dot_general | solution.py:141
  130.2 0.1 reduce_max.29
  130.3 0.1 multiply_reduce_fusion.2
  130.4 0.1 copy.69
  130.5 0.1 mul.364
  130.6 1.4 copy.70
  132.0 0.1 copy.71
  132.1 0.1 broadcast_multiply_fusion
  132.2 0.1 mul.370
  132.2 0.1 copy.73
  132.3 0.1 div.48
  132.4 0.1 div.49
  132.5 17.5 %all-to-all-done = f32[64,8,320]{2,1,0:T(8,128)S(1)} async-done(((f32[64,8,320]{2,1,0:T(8,128)}), f32[64,8,320]{2,1,0:T(8,128)S(1)}, u32[]{:S(2)}, u32[]{:S(2)}) %all-to-all-start) | async-done | bytes 655392 | tf_op jit(solution)/shard_map/all_to_all | solution.py:106
  149.9 1.3 multiply_reduce_fusion
  151.2 0.1 multiply_reduce_fusion.6
  151.4 7.7 %all-reduce = (f32[8]{0:T(128)S(1)}, f32[8]{0:T(128)S(1)}) all-reduce(f32[8]{0:T(128)S(1)} %get-tuple-element.6, f32[8]{0:T(128)S(1)} %get-tuple-element.36), channel_id=1, replica_groups=mesh['req'=64,'tp'=4] {'tp'}, use_global_device_ids=true, to_apply=%region_9.10 | all-reduce | flops 16 | bytes 128 | tf_op jit(solution)/shard_map/psum | solution.py:172
  159.1 0.3 convolution_divide_fusion.1
  159.4 0.3 fusion.7
  159.7 1.2 copy.74
  160.9 22.4 %reduce-scatter.4.cloned.1.call-done = f32[400,8]{1,0:T(8,128)} async-done(((f32[1600,8]{1,0:T(8,128)}), f32[400,8]{1,0:T(8,128)}) %reduce-scatter.4.cloned.1.call-update) | async-done | bytes 12816
  183.3 1.0 copy.75
  184.3 0.7 add_convert_fusion
  (50 shorter events, 0.5 us)
Async XLA Ops:
  7.2 152.2 %copy-start = (bf16[400,1600]{1,0:T(8,128)(2,1)S(1)}, bf16[400,1600]{1,0:T(8,128)(2,1)}, u32[]{:S(2)}) copy-start(bf16[400,1600]{1,0:T(8,128)(2,1)} %param.37) | copy-start | bytes 3840004
  7.2 57.2 %copy-start.1 = (s32[512]{0:T(512)S(1)}, s32[512]{0:T(512)}, u32[]{:S(2)}) copy-start(s32[512]{0:T(512)} %param.39) | copy-start | bytes 6148
  11.9 54.0 %copy-start.10 = (s32[34]{0:T(128)S(1)}, s32[34]{0:T(128)}, u32[]{:S(2)}) copy-start(s32[34]{0:T(128)} %param.40) | copy-start | bytes 412
  11.9 54.0 %copy-start.14 = (s32[34]{0:T(128)S(1)}, s32[34]{0:T(128)}, u32[]{:S(2)}) copy-start(s32[34]{0:T(128)} %param.41) | copy-start | bytes 412
  72.1 27.5 %all-to-all-start.2 = ((f32[64,8,5]{1,2,0:T(8,128)}), f32[64,8,5]{1,2,0:T(8,128)S(1)}, u32[]{:S(2)}, u32[]{:S(2)}) async-start(f32[64,8,5]{1,2,0:T(8,128)} %copy.72), calls=%async_computation.2 | async-start | bytes 524288 | tf_op jit(solution)/shard_map/all_to_all | solution.py:113
  80.2 3.9 %copy-start.9 = (f32[4,400]{1,0:T(4,128)S(1)}, f32[4,400]{1,0:T(4,128)}, u32[]{:S(2)}) copy-start(f32[4,400]{1,0:T(4,128)} %param.28) | copy-start | bytes 19204
  80.3 3.9 %copy-start.3 = (bf16[8,1600]{1,0:T(8,128)(2,1)S(1)}, bf16[8,1600]{1,0:T(8,128)(2,1)}, u32[]{:S(2)}) copy-start(bf16[8,1600]{1,0:T(8,128)(2,1)} %param.21) | copy-start | bytes 76804
  80.3 3.9 %copy-start.7 = (f32[1600]{0:T(1024)S(1)}, f32[1600]{0:T(1024)}, u32[]{:S(2)}) copy-start(f32[1600]{0:T(1024)} %param.22) | copy-start | bytes 19204
  84.0 2.1 %copy-start.5 = (bf16[400,132]{0,1:T(8,128)(2,1)S(1)}, bf16[400,132]{0,1:T(8,128)(2,1)}, u32[]{:S(2)}) copy-start(bf16[400,132]{0,1:T(8,128)(2,1)} %param.30) | copy-start | bytes 316804
  84.1 14.3 %copy-start.6 = (bf16[100,400]{0,1:T(8,128)(2,1)S(1)}, bf16[100,400]{0,1:T(8,128)(2,1)}, u32[]{:S(2)}) copy-start(bf16[100,400]{0,1:T(8,128)(2,1)} %param.31) | copy-start | bytes 240004
  84.1 14.3 %copy-start.11 = (f32[400]{0:T(512)S(1)}, f32[400]{0:T(512)}, u32[]{:S(2)}) copy-start(f32[400]{0:T(512)} %param.32) | copy-start | bytes 4804
  84.2 15.5 %copy-start.8 = (f32[16,400]{1,0:T(8,128)S(1)}, f32[16,400]{1,0:T(8,128)}, u32[]{:S(2)}) copy-start(f32[16,400]{1,0:T(8,128)} %param.33) | copy-start | bytes 76804
  86.1 24.0 %copy-start.4 = (f32[8,16,400]{2,1,0:T(8,128)S(1)}, f32[8,16,400]{2,1,0:T(8,128)}, u32[]{:S(2)}) copy-start(f32[8,16,400]{2,1,0:T(8,128)} %param.35) | copy-start | bytes 614404
  99.7 28.6 %copy-start.15 = (f32[400]{0:T(512)S(1)}, f32[400]{0:T(512)}, u32[]{:S(2)}) copy-start(f32[400]{0:T(512)} %param.34) | copy-start | bytes 4804
  99.7 21.9 %all-to-all-start.1 = ((f32[64,8,5]{1,2,0:T(8,128)}), f32[64,8,5]{1,2,0:T(8,128)S(1)}, u32[]{:S(2)}, u32[]{:S(2)}) async-start(f32[64,8,5]{1,2,0:T(8,128)} %copy.67), calls=%async_computation.1 | async-start | bytes 524288 | tf_op jit(solution)/shard_map/all_to_all | solution.py:120
  121.6 28.4 %all-to-all-start = ((f32[64,8,320]{2,1,0:T(8,128)}), f32[64,8,320]{2,1,0:T(8,128)S(1)}, u32[]{:S(2)}, u32[]{:S(2)}) async-start(f32[64,8,320]{2,1,0:T(8,128)} %fusion.41), calls=%async_computation | async-start | bytes 1572864 | tf_op jit(solution)/shard_map/all_to_all | solution.py:106
  128.1 55.2 %reduce-scatter.4.cloned.1.call-start = ((), (), s32[]{:S(2)}) async-start(), calls=%async_computation.4 | async-start | bytes 1024000
  132.0 27.1 %copy-start.2 = (bf16[320,1600]{1,0:T(8,128)(2,1)S(1)}, bf16[320,1600]{1,0:T(8,128)(2,1)}, u32[]{:S(2)}) copy-start(bf16[320,1600]{1,0:T(8,128)(2,1)} %param.25) | copy-start | bytes 3072004
  132.0 27.1 %copy-start.12 = (f32[320]{0:T(512)S(1)}, f32[320]{0:T(512)}, u32[]{:S(2)}) copy-start(f32[320]{0:T(512)} %param.26) | copy-start | bytes 3844
  132.5 26.9 %copy-start.13 = (f32[400]{0:T(512)S(1)}, f32[400]{0:T(512)}, u32[]{:S(2)}) copy-start(f32[400]{0:T(512)} %param.36) | copy-start | bytes 4804
Sparse Core Ops, SparseCore 0:
  161.0 22.2 reduce-scatter.3
where the time goes:
time: 193 us; the launch traced here: 192 us
  blocking collectives  68.9 us (36%)
  waiting for transfers between devices  50.5 us (26%)
  starting transfers between devices  25 us (13%)
  matrix products  16.5 us (9%)
  between operations  14.4 us (7%)
  local copies, waits for them, and re-layouts  8.94 us (5%)
  other arithmetic  7.63 us (4%)
    all_gather x1, blocking collectives, body(): lax.all_gather(query.reshape(row_count, head_count * head_dim), 'req', ax...  50.3 us
    unnamed x2, waiting for transfers between devices  22.4 us
    all_to_all x1, waiting for transfers between devices, body(): lax.all_to_all(part_out.reshape(holders, row_count, head_count * head_dim...  17.5 us
    psum x1, blocking collectives, body(): lax.psum(jnp.dot(activated, select_weight, preferred_element_type=jnp.flo...  10.8 us
    all_to_all x1, waiting for transfers between devices, body(): lax.all_to_all(request_max.reshape(holders, row_count, head_count), 'req'...  10.7 us
    all_to_all x1, starting transfers between devices, body(): lax.all_to_all(request_max.reshape(holders, row_count, head_count), 'req'...  10.3 us
    all_to_all x1, starting transfers between devices, body(): lax.all_to_all(part_sum.reshape(holders, row_count, head_count), 'req', s...  8.09 us
    psum x1, blocking collectives, body(): attn_total, mamba_total = lax.psum((attn_square, mamba_square), 'tp')  7.74 us
  transfers between devices with their start and end apart: 4, of which 3 were waited for; matrix products, arithmetic and copies ran while one was open for 7% of the time, Pallas kernels for 0%

commit v1 on v0

--- a/solution.py
+++ b/solution.py
@@ -70,9 +70,9 @@
     memory = jnp.dot(normed, memory_weight, preferred_element_type=jnp.float32)
     key_new = rotate_pairs(memory[:, None, :head_dim], own_len).astype(jnp.bfloat16)
     value_new = memory[:, head_dim:].astype(jnp.bfloat16)
-    all_query = lax.all_gather(
-        query.reshape(row_count, head_count * head_dim), "req", axis=0, tiled=True
-    )
+    own = query.reshape(row_count, head_count * head_dim)
+    repeated = jnp.stack([own] * lax.axis_size("req"))
+    all_query = jnp.concatenate(lax.all_to_all(repeated, "req", 0, 0), axis=0)
     slot_used = slot_request >= 0
     owner_row = jnp.where(slot_used, slot_request, 0)
     slot_query = jnp.take(all_query, owner_row, axis=0).reshape(slot_count, head_count, head_dim)

time: 193 us -> 159 us (0.82)
  blocking collectives: 68.9 us -> 18.6 us
  starting transfers between devices: 25 us -> 35.5 us
  waiting for transfers between devices: 50.5 us -> 56.8 us
    all_gather x1 -> x0, blocking collectives: 50.3 us -> none  [body(): lax.all_gather(query.reshape(row_count, head_count * head_dim), 'req', ax...]
    all_to_all x0 -> x1, starting transfers between devices: none -> 12.2 us  [body(): all_query = jnp.concatenate(lax.all_to_all(repeated, 'req', 0, 0), axis=0)]
    all_to_all x1, waiting for transfers between devices: 0.01 us -> 6.8 us  [body(): lax.all_to_all(part_sum.reshape(holders, row_count, head_count), 'req', s...]
    all_to_all x1, starting transfers between devices: 10.3 us -> 6.49 us  [body(): lax.all_to_all(request_max.reshape(holders, row_count, head_count), 'req'...]
    all_to_all x1, starting transfers between devices: 8.09 us -> 10.3 us  [body(): lax.all_to_all(part_sum.reshape(holders, row_count, head_count), 'req', s...]
  transfers between devices with their start and end apart: 4 -> 5, of which waited for: 3 -> 4; matrix products, arithmetic and copies ran while one was open for 7% -> 9% of each run, Pallas kernels for 0% -> 0%
where the time goes in v1:
time: 159 us; the launch traced here: 158 us
  waiting for transfers between devices  56.8 us (36%)
  starting transfers between devices  35.5 us (22%)
  blocking collectives  18.6 us (12%)
  matrix products  16.5 us (10%)
  between operations  14.4 us (9%)
  local copies, waits for them, and re-layouts  9.73 us (6%)
  other arithmetic  6.36 us (4%)
    unnamed x2, waiting for transfers between devices  22.4 us
    all_to_all x1, waiting for transfers between devices, body(): lax.all_to_all(part_out.reshape(holders, row_count, head_count * head_dim...  17.5 us
    all_to_all x1, starting transfers between devices, body(): all_query = jnp.concatenate(lax.all_to_all(repeated, 'req', 0, 0), axis=0)  12.2 us
    psum x1, blocking collectives, body(): lax.psum(jnp.dot(activated, select_weight, preferred_element_type=jnp.flo...  10.8 us
    all_to_all x1, starting transfers between devices, body(): lax.all_to_all(part_sum.reshape(holders, row_count, head_count), 'req', s...  10.3 us
    all_to_all x1, waiting for transfers between devices, body(): lax.all_to_all(request_max.reshape(holders, row_count, head_count), 'req'...  10.1 us
    psum x1, blocking collectives, body(): attn_total, mamba_total = lax.psum((attn_square, mamba_square), 'tp')  7.74 us
    all_to_all x1, waiting for transfers between devices, body(): lax.all_to_all(part_sum.reshape(holders, row_count, head_count), 'req', s...  6.8 us
  transfers between devices with their start and end apart: 5, of which 4 were waited for; matrix products, arithmetic and copies ran while one was open for 9% of the time, Pallas kernels for 0%

profile of v1, /device:TPU:2, one launch (start us, length us, event | category | flops | bytes accessed | tf_op | source)
XLA Modules:
  0.0 157.9 jit_solution(17377567592609342714)
XLA Ops:
  7.2 1.0 multiply_reduce_fusion.3
  8.2 1.3 fusion.74
  9.5 0.8 dynamic-slice_convert_fusion
  10.3 0.1 multiply_cosine_fusion.1
  10.4 0.1 fusion.65
  10.6 1.7 %fusion.69 = f32[8,320]{1,0:T(8,128)S(1)} fusion(bf16[1600,320]{0,1:T(8,128)(2,1)} %param.23, f32[1600]{0:T(1024)} %param.22, f32[8]{0:T(128)S(1)} %add_rsqrt_fusion, bf16[8,1600]{1,0:T(8,128)(2,1)} %param.21), kind=kOutput, calls=%fused_computation.104 | convolution fusion | flops 8243200 | bytes 1066272 | tf_op jit(solution)/shard_map/dot_general | solution.py:66
  12.2 0.1 reshape.307
  12.4 0.1 multiply_subtract_fusion
  12.5 0.2 multiply_reduce_fusion.4
  12.6 0.1 convert_element_type.90
  12.7 0.8 stack.3
  13.5 12.2 %all-to-all-start = ((bf16[64,8,320]{2,1,0:T(8,128)(2,1)}), bf16[64,8,320]{2,1,0:T(8,128)(2,1)S(1)}, u32[]{:S(2)}, u32[]{:S(2)}) async-start(bf16[64,8,320]{2,1,0:T(8,128)(2,1)} %stack.3), calls=%async_computation | async-start | bytes 786432 | tf_op jit(solution)/shard_map/all_to_all | solution.py:75
  25.8 0.1 iota_compare_fusion
  25.9 0.8 gather_fusion
  26.7 0.1 iota_compare_fusion.1
  26.8 1.8 %fusion.75 = (f32[8,400]{1,0:T(8,128)S(1)}, bf16[8,400]{1,0:T(8,128)(2,1)S(1)}) fusion(bf16[8,3,400]{2,0,1:T(8,128)(2,1)} %param.29, f32[400]{0:T(512)S(1)} %bitcast.83, f32[400]{0:T(512)S(1)} %bitcast.84, f32[400]{0:T(512)S(1)} %bitcast.82, bf16[2,1600,400]{1,2,0:T(8,128)(2,1)} %param.27, f32[1600]{0:T(1024)S(1)} %copy-done.7, f32[8]{0:T(128)S(1)} %add_rsqrt_fusion, ...), kind=kOutput, calls=%fused_computation.110 | convolution fusion | flops 10348800 | bytes 1413408 | tf_op jit(solution)/shard_map/dot_general | solution.py:138
  28.7 0.1 fusion.77
  28.8 10.8 %psum.22 = f32[8,132]{1,0:T(8,128)S(1)} all-reduce(f32[8,132]{1,0:T(8,128)S(1)} %fusion.77), channel_id=1, replica_groups=mesh['req'=64,'tp'=4] {'tp'}, use_global_device_ids=true, to_apply=%region_10.11 | all-reduce | flops 1056 | bytes 8448 | tf_op jit(solution)/shard_map/psum | solution.py:147
  39.8 0.2 fusion.76
  40.0 0.9 multiply_reduce_fusion.1
  40.8 0.6 gather_fusion.1
  41.5 0.1 gather.16
  41.6 3.6 %fusion.73 = (f32[34,5]{1,0:T(8,128)S(1)}, f32[34,5,512]{2,1,0:T(8,128)S(1)}) fusion(bf16[34,1,512,128]{3,2,1,0:T(8,128)(2,1)} %param.38, bf16[34,5,64]{2,1,0:T(8,128)(2,1)S(1)} %gather.16, pred[34]{0:T(512)(128)(4,1)S(1)} %get-tuple-element.14, pred[34,512]{1,0:T(8,128)(4,1)S(1)} %iota_compare_fusion.1), kind=kOutput, calls=%fused_computation.108 | convolution fusion | flops 11412950 | bytes 4844490 | tf_op jit(solution)/shard_map/shd,std->sht/dot_general | solution.py:83
  45.2 0.1 copy.65
  45.3 0.1 select_reduce_fusion
  45.5 0.1 copy.66
  45.6 0.6 gather_fusion.2
  46.2 0.1 subtract_exponential_fusion.1
  46.3 0.3 convert_reduce_fusion
  46.6 0.2 fusion.48
  46.8 0.1 reshape.311
  46.9 0.8 copy.72
  47.7 10.3 %all-to-all-start.3 = ((f32[64,8,5]{1,2,0:T(8,128)}), f32[64,8,5]{1,2,0:T(8,128)S(1)}, u32[]{:S(2)}, u32[]{:S(2)}) async-start(f32[64,8,5]{1,2,0:T(8,128)} %copy.72), calls=%async_computation.3 | async-start | bytes 524288 | tf_op jit(solution)/shard_map/all_to_all | solution.py:113
  58.1 3.7 %fusion.20 = f32[34,5,64]{2,1,0:T(8,128)S(1)} fusion(bf16[34,1,512,128]{3,2,1,0:T(8,128)(2,1)} %param.38, f32[34,5]{1,0:T(8,128)S(1)} %subtract_exponential_fusion.1, f32[34,5,512]{2,1,0:T(8,128)S(1)} %get-tuple-element.29, f32[34,5]{1,0:T(8,128)S(1)} %get-tuple-element.28, pred[34,512]{1,0:T(8,128)(4,1)S(1)} %iota_compare_fusion.1), kind=kOutput, calls=%fused_computation.21 | convolution fusion | flops 11413120 | bytes 4866896 | tf_op jit(solution)/shard_map/sht,std->shd/dot_general | solution.py:92
  61.8 0.1 reshape.310
  61.9 0.8 copy.67
  62.7 0.1 reshape.342
  62.8 6.8 %all-to-all-done.3 = f32[64,8,5]{1,2,0:T(8,128)S(1)} async-done(((f32[64,8,5]{1,2,0:T(8,128)}), f32[64,8,5]{1,2,0:T(8,128)S(1)}, u32[]{:S(2)}, u32[]{:S(2)}) %all-to-all-start.3) | async-done | bytes 10272 | tf_op jit(solution)/shard_map/all_to_all | solution.py:113
  69.6 6.5 %all-to-all-start.2 = ((f32[64,8,5]{1,2,0:T(8,128)}), f32[64,8,5]{1,2,0:T(8,128)S(1)}, u32[]{:S(2)}, u32[]{:S(2)}) async-start(f32[64,8,5]{1,2,0:T(8,128)} %copy.67), calls=%async_computation.2 | async-start | bytes 524288 | tf_op jit(solution)/shard_map/all_to_all | solution.py:120
  76.1 1.4 fusion.41
  77.5 10.1 %all-to-all-done.2 = f32[64,8,5]{1,2,0:T(8,128)S(1)} async-done(((f32[64,8,5]{1,2,0:T(8,128)}), f32[64,8,5]{1,2,0:T(8,128)S(1)}, u32[]{:S(2)}, u32[]{:S(2)}) %all-to-all-start.2) | async-done | bytes 10272 | tf_op jit(solution)/shard_map/all_to_all | solution.py:120
  87.6 6.5 %all-to-all-start.1 = ((f32[64,8,320]{2,1,0:T(8,128)}), f32[64,8,320]{2,1,0:T(8,128)S(1)}, u32[]{:S(2)}, u32[]{:S(2)}) async-start(f32[64,8,320]{2,1,0:T(8,128)} %fusion.41), calls=%async_computation.1 | async-start | bytes 1572864 | tf_op jit(solution)/shard_map/all_to_all | solution.py:106
  94.3 0.1 copy.68
  94.3 1.9 %multiply_reduce_fusion.5 = (f32[8]{0:T(128)S(1)}, f32[8,400]{1,0:T(8,128)S(1)}) fusion(bf16[2,1600,400]{1,2,0:T(8,128)(2,1)} %param.27, f32[1600]{0:T(1024)S(1)} %copy-done.7, f32[8]{0:T(128)S(1)} %add_rsqrt_fusion, bf16[8,1600]{1,0:T(8,128)(2,1)S(1)} %copy-done.3, f32[8,400]{1,0:T(8,128)S(1)} %get-tuple-element.4, ...), kind=kOutput, calls=%fused_computation.61 | convolution fusion | flops 10323192 | bytes 1396864 | tf_op jit(solution)/shard_map/dot_general | solution.py:141
  96.3 0.1 reduce_max.29
  96.4 0.1 multiply_reduce_fusion.2
  96.4 0.1 copy.69
  96.6 0.1 mul.364
  96.7 1.4 copy.70
  98.1 0.1 copy.71
  98.1 0.1 broadcast_multiply_fusion
  98.2 0.1 mul.370
  98.3 0.1 copy.73
  98.4 0.1 div.49
  98.5 17.5 %all-to-all-done.1 = f32[64,8,320]{2,1,0:T(8,128)S(1)} async-done(((f32[64,8,320]{2,1,0:T(8,128)}), f32[64,8,320]{2,1,0:T(8,128)S(1)}, u32[]{:S(2)}, u32[]{:S(2)}) %all-to-all-start.1) | async-done | bytes 655392 | tf_op jit(solution)/shard_map/all_to_all | solution.py:106
  116.0 1.3 multiply_reduce_fusion
  117.3 0.1 multiply_reduce_fusion.6
  117.4 7.7 %all-reduce = (f32[8]{0:T(128)S(1)}, f32[8]{0:T(128)S(1)}) all-reduce(f32[8]{0:T(128)S(1)} %get-tuple-element.6, f32[8]{0:T(128)S(1)} %get-tuple-element.36), channel_id=1, replica_groups=mesh['req'=64,'tp'=4] {'tp'}, use_global_device_ids=true, to_apply=%region_9.10 | all-reduce | flops 16 | bytes 128 | tf_op jit(solution)/shard_map/psum | solution.py:172
  125.2 0.3 convolution_divide_fusion.1
  125.5 0.3 fusion.7
  125.7 1.2 copy.74
  127.0 22.4 %reduce-scatter.4.cloned.1.call-done = f32[400,8]{1,0:T(8,128)} async-done(((f32[1600,8]{1,0:T(8,128)}), f32[400,8]{1,0:T(8,128)}) %reduce-scatter.4.cloned.1.call-update) | async-done | bytes 12816
  149.4 1.0 copy.75
  150.4 0.7 add_convert_fusion
  (52 shorter events, 0.6 us)
Async XLA Ops:
  7.2 118.3 %copy-start = (bf16[400,1600]{1,0:T(8,128)(2,1)S(1)}, bf16[400,1600]{1,0:T(8,128)(2,1)}, u32[]{:S(2)}) copy-start(bf16[400,1600]{1,0:T(8,128)(2,1)} %param.37) | copy-start | bytes 3840004
  9.4 16.3 %copy-start.10 = (s32[34]{0:T(128)S(1)}, s32[34]{0:T(128)}, u32[]{:S(2)}) copy-start(s32[34]{0:T(128)} %param.40) | copy-start | bytes 412
  9.4 16.4 %copy-start.1 = (s32[512]{0:T(512)S(1)}, s32[512]{0:T(512)}, u32[]{:S(2)}) copy-start(s32[512]{0:T(512)} %param.39) | copy-start | bytes 6148
  10.5 16.2 %copy-start.14 = (s32[34]{0:T(128)S(1)}, s32[34]{0:T(128)}, u32[]{:S(2)}) copy-start(s32[34]{0:T(128)} %param.41) | copy-start | bytes 412
  10.5 16.3 %copy-start.9 = (f32[4,400]{1,0:T(4,128)S(1)}, f32[4,400]{1,0:T(4,128)}, u32[]{:S(2)}) copy-start(f32[4,400]{1,0:T(4,128)} %param.28) | copy-start | bytes 19204
  10.5 16.3 %copy-start.3 = (bf16[8,1600]{1,0:T(8,128)(2,1)S(1)}, bf16[8,1600]{1,0:T(8,128)(2,1)}, u32[]{:S(2)}) copy-start(bf16[8,1600]{1,0:T(8,128)(2,1)} %param.21) | copy-start | bytes 76804
  10.5 16.3 %copy-start.7 = (f32[1600]{0:T(1024)S(1)}, f32[1600]{0:T(1024)}, u32[]{:S(2)}) copy-start(f32[1600]{0:T(1024)} %param.22) | copy-start | bytes 19204
  13.5 15.2 %copy-start.5 = (bf16[400,132]{0,1:T(8,128)(2,1)S(1)}, bf16[400,132]{0,1:T(8,128)(2,1)}, u32[]{:S(2)}) copy-start(bf16[400,132]{0,1:T(8,128)(2,1)} %param.30) | copy-start | bytes 316804
  13.5 27.3 %all-to-all-start = ((bf16[64,8,320]{2,1,0:T(8,128)(2,1)}), bf16[64,8,320]{2,1,0:T(8,128)(2,1)S(1)}, u32[]{:S(2)}, u32[]{:S(2)}) async-start(bf16[64,8,320]{2,1,0:T(8,128)(2,1)} %stack.3), calls=%async_computation | async-start | bytes 786432 | tf_op jit(solution)/shard_map/all_to_all | solution.py:75
  25.7 14.0 %copy-start.8 = (f32[16,400]{1,0:T(8,128)S(1)}, f32[16,400]{1,0:T(8,128)}, u32[]{:S(2)}) copy-start(f32[16,400]{1,0:T(8,128)} %param.33) | copy-start | bytes 76804
  25.7 14.1 %copy-start.6 = (bf16[100,400]{0,1:T(8,128)(2,1)S(1)}, bf16[100,400]{0,1:T(8,128)(2,1)}, u32[]{:S(2)}) copy-start(bf16[100,400]{0,1:T(8,128)(2,1)} %param.31) | copy-start | bytes 240004
  25.7 14.1 %copy-start.11 = (f32[400]{0:T(512)S(1)}, f32[400]{0:T(512)}, u32[]{:S(2)}) copy-start(f32[400]{0:T(512)} %param.32) | copy-start | bytes 4804
  25.7 14.2 %copy-start.4 = (f32[8,16,400]{2,1,0:T(8,128)S(1)}, f32[8,16,400]{2,1,0:T(8,128)}, u32[]{:S(2)}) copy-start(f32[8,16,400]{2,1,0:T(8,128)} %param.35) | copy-start | bytes 614404
  47.7 21.9 %all-to-all-start.3 = ((f32[64,8,5]{1,2,0:T(8,128)}), f32[64,8,5]{1,2,0:T(8,128)S(1)}, u32[]{:S(2)}, u32[]{:S(2)}) async-start(f32[64,8,5]{1,2,0:T(8,128)} %copy.72), calls=%async_computation.3 | async-start | bytes 524288 | tf_op jit(solution)/shard_map/all_to_all | solution.py:113
  69.6 18.0 %all-to-all-start.2 = ((f32[64,8,5]{1,2,0:T(8,128)}), f32[64,8,5]{1,2,0:T(8,128)S(1)}, u32[]{:S(2)}, u32[]{:S(2)}) async-start(f32[64,8,5]{1,2,0:T(8,128)} %copy.67), calls=%async_computation.2 | async-start | bytes 524288 | tf_op jit(solution)/shard_map/all_to_all | solution.py:120
  76.1 18.2 %copy-start.15 = (f32[400]{0:T(512)S(1)}, f32[400]{0:T(512)}, u32[]{:S(2)}) copy-start(f32[400]{0:T(512)} %param.34) | copy-start | bytes 4804
  87.6 28.4 %all-to-all-start.1 = ((f32[64,8,320]{2,1,0:T(8,128)}), f32[64,8,320]{2,1,0:T(8,128)S(1)}, u32[]{:S(2)}, u32[]{:S(2)}) async-start(f32[64,8,320]{2,1,0:T(8,128)} %fusion.41), calls=%async_computation.1 | async-start | bytes 1572864 | tf_op jit(solution)/shard_map/all_to_all | solution.py:106
  94.1 55.2 %reduce-scatter.4.cloned.1.call-start = ((), (), s32[]{:S(2)}) async-start(), calls=%async_computation.5 | async-start | bytes 1024000
  98.0 27.1 %copy-start.2 = (bf16[320,1600]{1,0:T(8,128)(2,1)S(1)}, bf16[320,1600]{1,0:T(8,128)(2,1)}, u32[]{:S(2)}) copy-start(bf16[320,1600]{1,0:T(8,128)(2,1)} %param.25) | copy-start | bytes 3072004
  98.0 27.1 %copy-start.12 = (f32[320]{0:T(512)S(1)}, f32[320]{0:T(512)}, u32[]{:S(2)}) copy-start(f32[320]{0:T(512)} %param.26) | copy-start | bytes 3844
  98.5 26.9 %copy-start.13 = (f32[400]{0:T(512)S(1)}, f32[400]{0:T(512)}, u32[]{:S(2)}) copy-start(f32[400]{0:T(512)} %param.36) | copy-start | bytes 4804
Sparse Core Ops, SparseCore 0:
  127.1 22.2 reduce-scatter.3
